TPU v7x, 32 devices: a whole 2x2x4 slice. The times are simulated.
32 devices in a mesh: groups: 2 (over y), hidden: 4 (over z), cols: 2 (over x), rep: 2 (over core).
Axes of the slice: x: 2, y: 2, z: 4, core: 2. Of those that a mesh axis runs over, the one named last changes fastest.
Arguments:
- inputs: bfloat16 [8192, 28672], P(('groups', 'cols', 'rep'), 'hidden'), parts along dimension 0, may hold values from -6 to 6
- grads: bfloat16 [8192, 8192], P(('groups', 'cols', 'rep'), 'hidden'), parts along dimension 0, may hold values from -1.5 to 1.5
- in_signs: int32 [28672], P('hidden'), may hold values from -1 to 1, as said below
- out_signs: int32 [8192], P('hidden'), may hold values from -1 to 1, as said below
- in_rows: int32 [128], replicated, may hold values from 0 to 28671, as said below
- out_rows: int32 [128], replicated, may hold values from 0 to 8191, as said below
- inv_gram: bfloat16 [16384, 16384], P('hidden', ('cols', 'rep')), may hold values from -0.0625 to 0.0625
Outputs:
- preconditioned: float32 [64, 16384], P('groups', ('cols', 'rep', 'hidden')), parts along dimension 0
There are 2 independent parts, one for each index of `groups`. A program takes and returns all parts, laid end to end along the dimension named above; an argument that names none is the same for every part. Nothing has to cross between parts.
Inputs may be any that keep to these rules, and one draw needn't show every extreme that they name: `in_signs`: each entry is -1 or +1. `out_signs`: each entry is -1 or +1. `in_rows`: distinct. `out_rows`: distinct.
All inputs are finite; a program needn't handle non-finite values.
Results may differ from a plain program's by a relative error of at most 0.0003.
Values sent between devices are 32-bit elements; how exact they have to be, the bound alone decides.
A program may use at most 128 MiB of HBM per device.

v0:
```python
import math

import jax
import jax.numpy as jnp
from jax import lax
from jax.sharding import PartitionSpec as P

IN_W = 28672
OUT_W = 8192
HAD = 64
SKETCH = 128
SEQ = 128


def had_sign(left, right):
    both = jnp.bitwise_and(left, right)
    count = jnp.zeros(both.shape, jnp.int32)
    for bit in range(HAD.bit_length() - 1):
        count = count + jnp.bitwise_and(jnp.right_shift(both, bit), 1)
    return (1 - 2 * (count % 2)).astype(jnp.float32)


def local_sketch(values, signs, rows, width, shard):
    inner = width // HAD
    local_high = values.shape[1] // inner
    row_high = rows // inner
    row_low = rows % inner
    cube = values.reshape(values.shape[0], local_high, inner)
    sign_grid = signs.reshape(local_high, inner)
    picked = jnp.take(cube, row_low, axis=2)
    sources = shard * local_high + jnp.arange(local_high, dtype=jnp.int32)
    coef = (
        had_sign(row_high[None, :], sources[:, None])
        * jnp.take(sign_grid, row_low, axis=1).astype(jnp.float32)
        / math.sqrt(HAD)
    )
    return jnp.einsum(
        "thk,hk->tk", picked, coef.astype(jnp.bfloat16), preferred_element_type=jnp.float32
    )


def on_device(inputs, grads, in_signs, out_signs, in_rows, out_rows, inv_gram):
    shard = lax.axis_index("hidden")
    out_part = local_sketch(grads, out_signs, out_rows, OUT_W, shard)
    in_part = local_sketch(inputs, in_signs, in_rows, IN_W, shard)
    block_p = inv_gram.shape[0] // SKETCH
    count = inputs.shape[0] // SEQ
    out_mine = lax.psum_scatter(out_part, "hidden", scatter_dimension=1, tiled=True)
    in_sketch = lax.psum(in_part, "hidden")
    projected = jnp.einsum(
        "esp,esq->epq",
        out_mine.reshape(count, SEQ, block_p),
        in_sketch.reshape(count, SEQ, SKETCH),
        precision=lax.Precision.HIGHEST,
    )
    projected = projected.reshape(count, block_p * SKETCH)
    tile_wide = inv_gram.astype(jnp.float32)
    partial_out = jnp.dot(
        lax.all_gather(projected, ("cols", "rep"), axis=0, tiled=True),
        tile_wide,
        precision=lax.Precision.HIGHEST,
        preferred_element_type=jnp.float32,
    )
    return lax.psum_scatter(partial_out, "hidden", scatter_dimension=1, tiled=True)


def solution(mesh):
    return jax.shard_map(
        on_device,
        mesh=mesh,
        in_specs=(
            P(("groups", "cols", "rep"), "hidden"),
            P(("groups", "cols", "rep"), "hidden"),
            P("hidden"),
            P("hidden"),
            P(),
            P(),
            P("hidden", ("cols", "rep")),
        ),
        out_specs=P("groups", ("cols", "rep", "hidden")),
        check_vma=False,
    )
```

profile of v0, /device:TPU:0, one launch (start us, length us, event | category | flops | bytes accessed | tf_op | source)
XLA Modules:
  0.0 182.0 jit_solution(4570917729813937851)
XLA Ops:
  6.5 0.0 all-reduce.2.cloned.1.call-start
  6.5 0.7 compare_and_fusion
  7.2 0.7 and_select_fusion.1
  7.9 0.8 reshape.40
  8.8 0.1 copy.24
  8.9 0.7 gather_fusion.2
  9.6 0.8 copy.20
  10.4 0.6 gather_fusion
  11.1 0.1 fusion.43
  11.2 0.1 copy.37
  11.3 20.0 %copy.26 = bf16[1024,7168]{0,1:T(8,128)(2,1)} copy(bf16[1024,7168]{1,0:T(8,128)(2,1)} %param.7) | data formatting | bytes 29360128 | tf_op args[0]
  31.3 16.7 %copy.27 = bf16[1024,16,448]{0,1,2:T(8,128)(2,1)} copy(bf16[1024,16,448]{0,2,1:T(8,128)(2,1)} %bitcast.46) | data formatting | bytes 29360128 | tf_op jit(solution)/shard_map/reshape | solution.py:28
  48.0 8.0 %gather_fusion.3 = bf16[128,1024,16]{1,2,0:T(8,128)(2,1)} fusion(bf16[1024,16,448]{0,1,2:T(8,128)(2,1)} %copy.27, s32[1024]{0:T(1024)S(1)} %pad_clamp_fusion), kind=kCustom, calls=%fused_computation.3 | custom fusion | bytes 8389120 | tf_op jit(solution)/shard_map/jit(_take)/gather | solution.py:30
  55.9 3.8 %multiply_reduce_fusion = f32[128,1024]{1,0:T(8,128)S(1)} fusion(f32[128,16]{1,0:T(8,128)S(1)} %copy.37, bf16[128,1024,16]{1,2,0:T(8,128)(2,1)} %gather_fusion.3, pred[128]{0:T(512)(128)(4,1)S(1)} %get-tuple-element.7), kind=kLoop, calls=%fused_computation.4 | loop fusion | flops 8257536 | bytes 4726912
  59.7 1.1 copy.36
  60.8 0.0 all-reduce.2.cloned.1.call-update
  60.8 0.0 reduce-scatter.3.cloned.1.call-start
  60.9 0.1 copy.29
  61.0 6.4 %copy.22 = bf16[1024,2048]{0,1:T(8,128)(2,1)} copy(bf16[1024,2048]{1,0:T(8,128)(2,1)} %param.8) | data formatting | bytes 8388608 | tf_op args[1]
  67.4 6.5 %copy.23 = bf16[1024,16,128]{0,1,2:T(8,128)(2,1)} copy(bf16[1024,16,128]{0,2,1:T(8,128)(2,1)} %bitcast.47) | data formatting | bytes 8388608 | tf_op jit(solution)/shard_map/reshape | solution.py:28
  73.9 5.0 %gather_fusion.1 = bf16[128,1024,16]{1,2,0:T(8,128)(2,1)} fusion(bf16[1024,16,128]{0,1,2:T(8,128)(2,1)} %copy.23, s32[1024]{0:T(1024)S(1)} %pad_clamp_fusion.1), kind=kCustom, calls=%fused_computation.1 | custom fusion | bytes 8389120 | tf_op jit(solution)/shard_map/jit(_take)/gather | solution.py:30
  78.9 3.0 %fusion = f32[128,1,1024]{2,1,0:T(1,128)S(1)} fusion(bf16[16,128,1]{0,2,1:T(2,128)(2,1)S(1)} %copy.29, bf16[128,1024,16]{1,2,0:T(8,128)(2,1)} %gather_fusion.1, pred[128]{0:T(512)(128)(4,1)S(1)} %get-tuple-element.11), kind=kOutput, calls=%fused_computation.5 | convolution fusion | flops 6291456 | bytes 4722816 | tf_op jit(solution)/shard_map/thk,hk->tk/dot_general | solution.py:37
  81.9 0.9 copy.46
  82.8 0.0 reduce-scatter.3.cloned.1.call-update
  82.8 0.0 reduce-scatter.5.cloned.1.call-start
  82.9 19.0 %all-reduce.2.cloned.1.call-done = f32[8,128,128]{2,1,0:T(8,128)} async-done(((f32[8,128,128]{2,1,0:T(8,128)}), f32[8,128,128]{2,1,0:T(8,128)}) %all-reduce.2.cloned.1.call-update) | async-done | bytes 524304 | tf_op jit(solution)/shard_map/psum | solution.py:49
  101.9 23.9 %reduce-scatter.3.cloned.1.call-done = f32[1024,32]{0,1:T(8,128)} async-done(((f32[1024,128]{0,1:T(8,128)}), f32[1024,32]{0,1:T(8,128)}) %reduce-scatter.3.cloned.1.call-update) | async-done | bytes 131088 | tf_op jit(solution)/shard_map/reduce_scatter | solution.py:48
  125.9 1.7 convolution_bitcast_fusion
  127.5 0.1 copy.47
  127.6 7.3 %all_gather.3 = f32[32,4096]{1,0:T(8,128)S(1)} all-gather(f32[8,4096]{1,0:T(8,128)S(1)} %bitcast.50), channel_id=1, replica_groups=mesh['groups'=2,'hidden'=4,'cols'=2,'rep'=2] {'cols','rep'}, dimensions={0}, use_global_device_ids=true | all-gather | bytes 655360 | tf_op jit(solution)/shard_map/all_gather | solution.py:59
  134.9 21.1 %fusion.45 = f32[32,4096]{1,0:T(8,128)} fusion(f32[32,4096]{1,0:T(8,128)S(1)} %all_gather.3, bf16[4096,4096]{1,0:T(8,128)(2,1)} %param.13), kind=kOutput, calls=%fused_computation.86 | convolution fusion | flops 6442450944 | bytes 34603008 | tf_op jit(solution)/shard_map/dot_general | solution.py:58
  155.9 0.0 reduce-scatter.5.cloned.1.call-update
  156.0 19.5 %reduce-scatter.5.cloned.1.call-done = f32[32,1024]{1,0:T(8,128)} async-done(((f32[32,4096]{1,0:T(8,128)}), f32[32,1024]{1,0:T(8,128)}) %reduce-scatter.5.cloned.1.call-update) | async-done | bytes 131088 | tf_op jit(solution)/shard_map/reduce_scatter | solution.py:64
  (5 shorter events, 0.1 us)
Async XLA Ops:
  6.5 95.4 %all-reduce.2.cloned.1.call-start = ((), (), s32[]{:S(2)}) async-start(), calls=%async_computation.3 | async-start | bytes 1048576 | tf_op jit(solution)/shard_map/psum | solution.py:49
  60.8 65.1 %reduce-scatter.3.cloned.1.call-start = ((), (), s32[]{:S(2)}) async-start(), calls=%async_computation.2 | async-start | bytes 655360 | tf_op jit(solution)/shard_map/reduce_scatter | solution.py:48
  82.8 92.6 %reduce-scatter.5.cloned.1.call-start = ((), (), s32[]{:S(2)}) async-start(), calls=%async_computation.4 | async-start | bytes 655360 | tf_op jit(solution)/shard_map/reduce_scatter | solution.py:64
Sparse Core Ops, SparseCore 0:
  60.9 40.9 all-reduce.1
  104.2 21.6 reduce-scatter.2
  156.1 19.2 reduce-scatter.4
where the time goes:
time: 183 us; the launch traced here: 182 us
  local copies, waits for them, and re-layouts  68 us (37%)
  waiting for transfers between devices  62.5 us (34%)
  matrix products  25.7 us (14%)
  between operations  13.2 us (7%)
  blocking collectives  7.28 us (4%)
  other arithmetic  5.26 us (3%)
    unnamed x4, local copies, waits for them, and re-layouts  26.6 us
    reduce_scatter x1, waiting for transfers between devices, on_device(): lax.psum_scatter(out_part, 'hidden', scatter_dimension=1, tiled=True)  23.9 us
    reshape x2, local copies, waits for them, and re-layouts, local_sketch(): cube = values.reshape(values.shape[0], local_high, inner)  23.2 us
    dot_general x1, matrix products, on_device(): jnp.dot(lax.all_gather(projected, ('cols', 'rep'), axis=0, tiled=True), t...  21.1 us
    reduce_scatter x1, waiting for transfers between devices, on_device(): lax.psum_scatter(partial_out, 'hidden', scatter_dimension=1, tiled=True)  19.5 us
    psum x1, waiting for transfers between devices, on_device(): in_sketch = lax.psum(in_part, 'hidden')  19 us
    gather x2, local copies, waits for them, and re-layouts, local_sketch(): picked = jnp.take(cube, row_low, axis=2)  13 us
    all_gather x1, blocking collectives, on_device(): lax.all_gather(projected, ('cols', 'rep'), axis=0, tiled=True)  7.28 us
  transfers between devices with their start and end apart: 3, of which 3 were waited for; matrix products, arithmetic and copies ran while one was open for 12% of the time, Pallas kernels for 0%

commit v1 on v0

v1 whole, which is shorter than its diff:
```python
import functools
import math

import jax
import jax.numpy as jnp
from jax import lax
from jax.experimental import pallas as pl
from jax.experimental.pallas import tpu as pltpu
from jax.sharding import PartitionSpec as P

IN_W = 28672
OUT_W = 8192
HAD = 64
SKETCH = 128
SEQ = 128
MESH = pl.DeviceIdType.MESH


def had_parity(left, right):
    both = jnp.bitwise_and(left, right)
    for shift in (4, 2, 1):
        both = jnp.bitwise_xor(both, jnp.right_shift(both, shift))
    return jnp.bitwise_and(both, 1)


def split_rows(rows, inner):
    high = jnp.floor((rows.astype(jnp.float32) + 0.5) * (1.0 / inner)).astype(jnp.int32)
    return high, rows - high * inner


def build_matrix(rows_ref, sign_ref, out_ref, shard, width):
    inner = width // HAD
    local_high = sign_ref.shape[0]
    high, low = split_rows(rows_ref[...], inner)
    hit = lax.broadcasted_iota(jnp.int32, (inner, SKETCH), 0) == low
    onehot = jnp.where(hit, 1.0, 0.0)
    picked = jnp.dot(
        sign_ref[...].astype(jnp.bfloat16),
        onehot.astype(jnp.bfloat16),
        preferred_element_type=jnp.float32,
    )
    sources = shard * local_high + lax.broadcasted_iota(jnp.int32, (local_high, SKETCH), 0)
    parity = had_parity(jnp.broadcast_to(high, (local_high, SKETCH)), sources)
    coef = picked * (1 - 2 * parity).astype(jnp.float32) * (1.0 / math.sqrt(HAD))
    for h in range(local_high):
        out_ref[h * inner : (h + 1) * inner, :] = (onehot * coef[h : h + 1, :]).astype(jnp.bfloat16)


def fused_kernel(
    dims,
    x_ref,
    g_ref,
    in_sign_ref,
    out_sign_ref,
    in_rows_ref,
    out_rows_ref,
    gram_ref,
    out_ref,
    x_buf,
    g_buf,
    gram_buf,
    mat_in,
    mat_out,
    part,
    land,
    proj,
    allp,
    wide,
    psum,
    final,
    x_sem,
    g_sem,
    gram_sem,
    send1,
    recv1,
    send2,
    recv2,
    send3,
    recv3,
    send4,
    recv4,
):
    hidden, cols, rep = dims
    me = lax.axis_index("hidden")
    my_col = lax.axis_index("cols")
    my_rep = lax.axis_index("rep")
    tokens = x_buf.shape[1]
    each = tokens // SEQ
    block_p = SKETCH // hidden
    peers = [(c, r) for c in range(cols) for r in range(rep) if (c, r) != (0, 0)]

    def to(k):
        return lax.rem(me + 1 + k, hidden)

    def source(k):
        return lax.rem(me + 2 * hidden - 1 - k, hidden)

    def load_x(k):
        row = pl.multiple_of(to(k) * tokens, tokens)
        return pltpu.make_async_copy(x_ref.at[pl.ds(row, tokens)], x_buf.at[k], x_sem.at[k])

    def load_g(k):
        row = pl.multiple_of(to(k) * tokens, tokens)
        return pltpu.make_async_copy(g_ref.at[pl.ds(row, tokens)], g_buf.at[k], g_sem.at[k])

    gram_parts = gram_sem.shape[0]
    gram_rows = gram_ref.shape[0] // gram_parts

    def load_gram(k):
        where = pl.ds(k * gram_rows, gram_rows)
        return pltpu.make_async_copy(gram_ref.at[where], gram_buf.at[where], gram_sem.at[k])

    for k in range(hidden):
        load_g(k).start()
        load_x(k).start()

    barrier = pltpu.get_barrier_semaphore()
    for k in range(hidden - 1):
        pl.semaphore_signal(barrier, inc=1, device_id={"hidden": to(k)}, device_id_type=MESH)
    for c, r in peers:
        pl.semaphore_signal(
            barrier,
            inc=1,
            device_id={"cols": lax.rem(my_col + c, cols), "rep": lax.rem(my_rep + r, rep)},
            device_id_type=MESH,
        )
    build_matrix(out_rows_ref, out_sign_ref, mat_out, me, OUT_W)
    build_matrix(in_rows_ref, in_sign_ref, mat_in, me, IN_W)
    pl.semaphore_wait(barrier, hidden - 1 + len(peers))

    def send_part(k):
        return pltpu.make_async_remote_copy(
            src_ref=part.at[k],
            dst_ref=land.at[k],
            send_sem=send1.at[k],
            recv_sem=recv1.at[k],
            device_id={"hidden": to(k)},
            device_id_type=MESH,
        )

    def sketch_step(k, carry):
        load_g(k).wait()
        part[k, 0] = jnp.dot(g_buf[k], mat_out[...], preferred_element_type=jnp.float32)
        load_x(k).wait()
        part[k, 1] = jnp.dot(x_buf[k], mat_in[...], preferred_element_type=jnp.float32)

        @pl.when(k < hidden - 1)
        def _():
            send_part(k).start()

        return carry

    lax.fori_loop(0, hidden, sketch_step, 0)
    for k in range(gram_parts):
        load_gram(k).start()
    for k in range(hidden - 1):
        send_part(k).wait_recv()

    for j in range(each):
        at = pl.ds(j * SEQ, SEQ)
        left = part[hidden - 1, 0, at, :]
        right = part[hidden - 1, 1, at, :]
        for k in range(hidden - 1):
            left = left + land[k, 0, at, :]
            right = right + land[k, 1, at, :]
        proj[j] = lax.dot_general(
            left,
            right,
            (((0,), (0,)), ((), ())),
            precision=lax.Precision.HIGHEST,
            preferred_element_type=jnp.float32,
        )

    mine = (my_col * rep + my_rep) * (hidden * each)

    def send_rows(k):
        return pltpu.make_async_remote_copy(
            src_ref=proj.at[:, pl.ds(pl.multiple_of(to(k) * block_p, block_p), block_p), :],
            dst_ref=allp.at[pl.ds(mine + me * each, each)],
            send_sem=send2.at[k],
            recv_sem=recv2.at[k],
            device_id={"hidden": to(k)},
            device_id_type=MESH,
        )

    def arrived_rows(k):
        return pltpu.make_async_remote_copy(
            src_ref=proj.at[:, pl.ds(0, block_p), :],
            dst_ref=allp.at[pl.ds(mine + source(k) * each, each)],
            send_sem=send2.at[k],
            recv_sem=recv2.at[k],
            device_id={"hidden": to(k)},
            device_id_type=MESH,
        )

    for k in range(hidden - 1):
        send_rows(k).start()
    for j in range(each):
        allp[mine + me * each + j] = proj[j, pl.ds(pl.multiple_of(me * block_p, block_p), block_p), :]

    def forward(d, k):
        c, r = peers[d]
        block = allp.at[pl.ds(mine + source(k) * each, each)]
        return pltpu.make_async_remote_copy(
            src_ref=block,
            dst_ref=block,
            send_sem=send3.at[d, k],
            recv_sem=recv3.at[d, k],
            device_id={"cols": lax.rem(my_col + c, cols), "rep": lax.rem(my_rep + r, rep)},
            device_id_type=MESH,
        )

    def forwarded(d, k):
        c, r = peers[d]
        col = lax.rem(my_col + cols - c, cols)
        other = (col * rep + lax.rem(my_rep + rep - r, rep)) * (hidden * each)
        block = allp.at[pl.ds(other + source(k) * each, each)]
        return pltpu.make_async_remote_copy(
            src_ref=block,
            dst_ref=block,
            send_sem=send3.at[d, k],
            recv_sem=recv3.at[d, k],
            device_id={"cols": col},
            device_id_type=MESH,
        )

    for d in range(len(peers)):
        forward(d, hidden - 1).start()
    for k in range(hidden - 1):
        arrived_rows(k).wait_recv()
        for d in range(len(peers)):
            forward(d, k).start()
    for k in range(hidden):
        for d in range(len(peers)):
            forwarded(d, k).wait_recv()

    examples = allp.shape[0]
    for p in range(block_p):
        rows = allp[:, p, :]
        upper = rows.astype(jnp.bfloat16)
        wide[0:examples, p * SKETCH : (p + 1) * SKETCH] = upper
        wide[examples:, p * SKETCH : (p + 1) * SKETCH] = (rows - upper.astype(jnp.float32)).astype(jnp.bfloat16)
    for k in range(gram_parts):
        load_gram(k).wait()

    share = psum.shape[2]
    step = 256
    per = share // step

    def send_sum(k):
        return pltpu.make_async_remote_copy(
            src_ref=psum.at[k],
            dst_ref=final.at[k],
            send_sem=send4.at[k],
            recv_sem=recv4.at[k],
            device_id={"hidden": to(k)},
            device_id_type=MESH,
        )

    def gram_step(n, carry):
        k = n // per
        at = pl.multiple_of(lax.rem(n, per) * step, step)
        column = pl.multiple_of(to(k) * share + at, step)
        both = jnp.dot(wide[...], gram_buf[:, pl.ds(column, step)], preferred_element_type=jnp.float32)
        psum[k, :, pl.ds(at, step)] = both[:examples] + both[examples:]

        @pl.when(jnp.logical_and(lax.rem(n, per) == per - 1, k < hidden - 1))
        def _():
            send_sum(k).start()

        return carry

    lax.fori_loop(0, hidden * per, gram_step, 0)
    total = psum[hidden - 1]
    for k in range(hidden - 1):
        send_sum(k).wait_recv()
        total = total + final[k]
    out_ref[...] = total

    for k in range(hidden - 1):
        send_part(k).wait_send()
        send_rows(k).wait_send()
        send_sum(k).wait_send()
    for k in range(hidden):
        for d in range(len(peers)):
            forward(d, k).wait_send()


def fused(dims, inputs, grads, in_signs, out_signs, in_rows, out_rows, inv_gram):
    hidden, cols, rep = dims
    tokens = inputs.shape[0] // hidden
    count = inputs.shape[0] // SEQ
    each = count // hidden
    block_p = SKETCH // hidden
    examples = count * cols * rep
    share = inv_gram.shape[1] // hidden
    others = cols * rep - 1
    f32 = jnp.float32
    dma = pltpu.SemaphoreType.DMA
    vmem = pl.BlockSpec(memory_space=pltpu.VMEM)
    hbm = pl.BlockSpec(memory_space=pl.ANY)
    gram_parts = 4
    return pl.pallas_call(
        functools.partial(fused_kernel, dims),
        out_shape=jax.ShapeDtypeStruct((examples, share), f32),
        in_specs=[hbm, hbm, vmem, vmem, vmem, vmem, hbm],
        out_specs=vmem,
        scratch_shapes=[
            pltpu.VMEM((hidden, tokens, inputs.shape[1]), jnp.bfloat16),
            pltpu.VMEM((hidden, tokens, grads.shape[1]), jnp.bfloat16),
            pltpu.VMEM(inv_gram.shape, jnp.bfloat16),
            pltpu.VMEM((inputs.shape[1], SKETCH), jnp.bfloat16),
            pltpu.VMEM((grads.shape[1], SKETCH), jnp.bfloat16),
            pltpu.VMEM((hidden, 2, tokens, SKETCH), f32),
            pltpu.VMEM((hidden - 1, 2, tokens, SKETCH), f32),
            pltpu.VMEM((each, SKETCH, SKETCH), f32),
            pltpu.VMEM((examples, block_p, SKETCH), f32),
            pltpu.VMEM((2 * examples, block_p * SKETCH), jnp.bfloat16),
            pltpu.VMEM((hidden, examples, share), f32),
            pltpu.VMEM((hidden - 1, examples, share), f32),
            dma((hidden,)),
            dma((hidden,)),
            dma((gram_parts,)),
            dma((hidden - 1,)),
            dma((hidden - 1,)),
            dma((hidden - 1,)),
            dma((hidden - 1,)),
            dma((others, hidden)),
            dma((others, hidden)),
            dma((hidden - 1,)),
            dma((hidden - 1,)),
        ],
        compiler_params=pltpu.CompilerParams(
            collective_id=0, has_side_effects=True, vmem_limit_bytes=63 << 20
        ),
    )(
        inputs,
        grads,
        in_signs.reshape(inputs.shape[1] // (IN_W // HAD), IN_W // HAD),
        out_signs.reshape(grads.shape[1] // (OUT_W // HAD), OUT_W // HAD),
        in_rows.reshape(1, SKETCH),
        out_rows.reshape(1, SKETCH),
        inv_gram,
    )


def plain_sketch(values, signs, rows, width, shard):
    inner = width // HAD
    local_high = values.shape[1] // inner
    high, low = rows // inner, rows % inner
    feature = jnp.arange(values.shape[1], dtype=jnp.int32)
    sources = shard * local_high + feature // inner
    sign = (1 - 2 * had_parity(high[None, :], sources[:, None])) * signs[:, None]
    hit = (feature % inner)[:, None] == low[None, :]
    matrix = jnp.where(hit, sign.astype(jnp.float32) / math.sqrt(HAD), 0.0)
    return jnp.dot(values, matrix.astype(jnp.bfloat16), preferred_element_type=jnp.float32)


def plain(inputs, grads, in_signs, out_signs, in_rows, out_rows, inv_gram):
    shard = lax.axis_index("hidden")
    out_part = plain_sketch(grads, out_signs, out_rows, OUT_W, shard)
    in_part = plain_sketch(inputs, in_signs, in_rows, IN_W, shard)
    block_p = inv_gram.shape[0] // SKETCH
    count = inputs.shape[0] // SEQ
    out_mine = lax.psum_scatter(out_part, "hidden", scatter_dimension=1, tiled=True)
    in_sketch = lax.psum(in_part, "hidden")
    projected = jnp.einsum(
        "esp,esq->epq",
        out_mine.reshape(count, SEQ, block_p),
        in_sketch.reshape(count, SEQ, SKETCH),
        precision=lax.Precision.HIGHEST,
    )
    projected = projected.reshape(count, block_p * SKETCH)
    partial_out = jnp.dot(
        lax.all_gather(projected, ("cols", "rep"), axis=0, tiled=True),
        inv_gram.astype(jnp.float32),
        precision=lax.Precision.HIGHEST,
        preferred_element_type=jnp.float32,
    )
    return lax.psum_scatter(partial_out, "hidden", scatter_dimension=1, tiled=True)


def solution(mesh):
    dims = tuple(mesh.shape[name] for name in ("hidden", "cols", "rep"))

    def on_device(inputs, *rest):
        if inputs.shape[0] % (dims[0] * SEQ) == 0:
            return fused(dims, inputs, *rest)
        return plain(inputs, *rest)

    return jax.shard_map(
        on_device,
        mesh=mesh,
        in_specs=(
            P(("groups", "cols", "rep"), "hidden"),
            P(("groups", "cols", "rep"), "hidden"),
            P("hidden"),
            P("hidden"),
            P(),
            P(),
            P("hidden", ("cols", "rep")),
        ),
        out_specs=P("groups", ("cols", "rep", "hidden")),
        check_vma=False,
    )
```

time: 183 us -> 60.4 us (0.33)
  local copies, waits for them, and re-layouts: 68 us -> 3 us
  waiting for transfers between devices: 62.5 us -> 0 us
  Pallas kernels: 0 us -> 57.1 us
  matrix products: 25.7 us -> 0 us
  between operations: 13.2 us -> 0.01 us
  blocking collectives: 7.28 us -> 0 us
  other arithmetic: 5.26 us -> 0 us
    pallas_call x0 -> x1, Pallas kernels: none -> 57.1 us  [fused(): pl.pallas_call(functools.partial(fused_kernel, dims), out_shape=jax.Shape...]
    reduce_scatter x2 -> x0, waiting for transfers between devices: 43.4 us -> none  [the longest x1 23.9 us: on_device(): lax.psum_scatter(out_part, 'hidden', scatter_dimension=1, tiled=True)]
    dot_general x3 -> x0, matrix products: 25.7 us -> none  [the longest x1 21.1 us: on_device(): jnp.dot(lax.all_gather(projected, ('cols', 'rep'), axis=0, tiled=True), t...]
    unnamed x4 -> x1, local copies, waits for them, and re-layouts: 26.6 us -> 1.57 us
    reshape x5 -> x1, local copies, waits for them, and re-layouts: 25 us -> 1.44 us  [fused(): in_signs.reshape(inputs.shape[1] // (IN_W // HAD), IN_W // HAD)]
    psum x1 -> x0, waiting for transfers between devices: 19 us -> none  [on_device(): in_sketch = lax.psum(in_part, 'hidden')]
    gather x6 -> x0, local copies, waits for them, and re-layouts: 14.3 us -> none  [the longest x2 13 us: local_sketch(): picked = jnp.take(cube, row_low, axis=2)]
    all_gather x1 -> x0, blocking collectives: 7.28 us -> none  [on_device(): lax.all_gather(projected, ('cols', 'rep'), axis=0, tiled=True)]
  transfers between devices with their start and end apart: 3 -> 0, of which waited for: 3 -> 0; matrix products, arithmetic and copies ran while one was open for 12% -> 0% of each run, Pallas kernels for 0% -> 0%
where the time goes in v1:
time: 60.4 us; the launch traced here: 60.1 us
  Pallas kernels  57.1 us (95%)
  local copies, waits for them, and re-layouts  3 us (5%)
    pallas_call x1, Pallas kernels, fused(): pl.pallas_call(functools.partial(fused_kernel, dims), out_shape=jax.Shape...  57.1 us
    unnamed x1, local copies, waits for them, and re-layouts  1.57 us
    reshape x1, local copies, waits for them, and re-layouts, fused(): in_signs.reshape(inputs.shape[1] // (IN_W // HAD), IN_W // HAD)  1.44 us

profile of v1, /device:TPU:0, one launch (start us, length us, event | category | flops | bytes accessed | tf_op | source)
XLA Modules:
  0.0 60.1 jit_solution(13489761622148858348)
XLA Ops:
  0.0 1.4 %reshape.12.in_sign_ref = s32[16,448]{1,0:T(8,128)} reshape(s32[7168]{0:T(1024)} %param.9) | data formatting | bytes 57344 | tf_op jit(solution)/shard_map/reshape | solution.py:339
  1.4 57.1 %shard_map.73 = f32[32,1024]{1,0:T(8,128)} custom-call(bf16[1024,7168]{1,0:T(8,128)(2,1)} %x_ref.1, bf16[1024,2048]{1,0:T(8,128)(2,1)} %g_ref.1, s32[16,448]{1,0:T(8,128)} %reshape.12.in_sign_ref, s32[16,128]{1,0:T(8,128)} %bitcast.3, s32[1,128]{1,0:T(1,128)} %bitcast.4, s32[1,128]{1,0:T(1,128)} %bitcast.5, bf16[4096,4096]{1,0:T(8,128)(2,1)} %gram_ref.1), custom_call_target="tpu_custom_call" | custom-call | tf_op jit(solution)/shard_map/pallas_call | solution.py:303
  58.5 1.6 %copy.9 = f32[32,1024]{1,0:T(8,128)} copy(f32[32,1024]{1,0:T(8,128)} %shard_map.73) | data formatting | bytes 262144

commit v2 on v1

--- a/solution.py
+++ b/solution.py
@@ -77,6 +77,8 @@
     recv2,
     send3,
     recv3,
+    send5,
+    recv5,
     send4,
     recv4,
 ):
@@ -87,7 +89,6 @@
     tokens = x_buf.shape[1]
     each = tokens // SEQ
     block_p = SKETCH // hidden
-    peers = [(c, r) for c in range(cols) for r in range(rep) if (c, r) != (0, 0)]
 
     def to(k):
         return lax.rem(me + 1 + k, hidden)
@@ -95,12 +96,17 @@
     def source(k):
         return lax.rem(me + 2 * hidden - 1 - k, hidden)
 
+    def target(s):
+        outer = 1 - lax.rem((me + 1) // 2, 2)
+        first = outer * (3 - s) + (1 - outer) * lax.rem(2 + 3 * s, 5)
+        return first + (me // 2) * (3 - 2 * first)
+
     def load_x(k):
-        row = pl.multiple_of(to(k) * tokens, tokens)
+        row = pl.multiple_of(target(k) * tokens, tokens)
         return pltpu.make_async_copy(x_ref.at[pl.ds(row, tokens)], x_buf.at[k], x_sem.at[k])
 
     def load_g(k):
-        row = pl.multiple_of(to(k) * tokens, tokens)
+        row = pl.multiple_of(target(k) * tokens, tokens)
         return pltpu.make_async_copy(g_ref.at[pl.ds(row, tokens)], g_buf.at[k], g_sem.at[k])
 
     gram_parts = gram_sem.shape[0]
@@ -117,122 +123,164 @@
     barrier = pltpu.get_barrier_semaphore()
     for k in range(hidden - 1):
         pl.semaphore_signal(barrier, inc=1, device_id={"hidden": to(k)}, device_id_type=MESH)
-    for c, r in peers:
-        pl.semaphore_signal(
-            barrier,
-            inc=1,
-            device_id={"cols": lax.rem(my_col + c, cols), "rep": lax.rem(my_rep + r, rep)},
-            device_id_type=MESH,
-        )
+    for c in range(1, cols):
+        pl.semaphore_signal(barrier, inc=1, device_id={"cols": lax.rem(my_col + c, cols)}, device_id_type=MESH)
+    for r in range(1, rep):
+        pl.semaphore_signal(barrier, inc=1, device_id={"rep": lax.rem(my_rep + r, rep)}, device_id_type=MESH)
     build_matrix(out_rows_ref, out_sign_ref, mat_out, me, OUT_W)
     build_matrix(in_rows_ref, in_sign_ref, mat_in, me, IN_W)
-    pl.semaphore_wait(barrier, hidden - 1 + len(peers))
-
-    def send_part(k):
-        return pltpu.make_async_remote_copy(
-            src_ref=part.at[k],
-            dst_ref=land.at[k],
-            send_sem=send1.at[k],
-            recv_sem=recv1.at[k],
-            device_id={"hidden": to(k)},
-            device_id_type=MESH,
-        )
-
-    def sketch_step(k, carry):
-        load_g(k).wait()
-        part[k, 0] = jnp.dot(g_buf[k], mat_out[...], preferred_element_type=jnp.float32)
-        load_x(k).wait()
-        part[k, 1] = jnp.dot(x_buf[k], mat_in[...], preferred_element_type=jnp.float32)
-
-        @pl.when(k < hidden - 1)
+    pl.semaphore_wait(barrier, hidden + cols + rep - 3)
+
+    edge = 1 - lax.rem((me + 1) // 2, 2)
+    half = me // 2
+    relay = hidden
+
+    def part_copy(s, j):
+        passed = edge * (1 - (s + hidden - 1) // hidden)
+        slot = me + passed * (relay - me)
+        dest = target(s)
+        return pltpu.make_async_remote_copy(
+            src_ref=part.at[s, j],
+            dst_ref=land.at[slot, j],
+            send_sem=send1.at[s, j],
+            recv_sem=recv1.at[slot, j],
+            device_id={"hidden": dest + passed * (1 + half - dest)},
+            device_id_type=MESH,
+        )
+
+    def part_arrived(slot, j):
+        return pltpu.make_async_remote_copy(
+            src_ref=part.at[0, j],
+            dst_ref=land.at[slot, j],
+            send_sem=send1.at[0, j],
+            recv_sem=recv1.at[slot, j],
+            device_id={"hidden": to(0)},
+            device_id_type=MESH,
+        )
+
+    def sketch_step(s, carry):
+        load_g(s).wait()
+        left = jnp.dot(g_buf[s], mat_out[...], preferred_element_type=jnp.float32)
+        load_x(s).wait()
+        right = jnp.dot(x_buf[s], mat_in[...], preferred_element_type=jnp.float32)
+        for j in range(each):
+            part[s, j, 0] = left[j * SEQ : (j + 1) * SEQ]
+            part[s, j, 1] = right[j * SEQ : (j + 1) * SEQ]
+
+        @pl.when(s < hidden - 2 + edge)
         def _():
-            send_part(k).start()
+            part_copy(s, 0).start()
 
         return carry
 
     lax.fori_loop(0, hidden, sketch_step, 0)
+    for j in range(1, each):
+        for s in range(hidden - 2):
+            part_copy(s, j).start()
+
+        @pl.when(edge == 1)
+        def _():
+            part_copy(hidden - 2, j).start()
+
     for k in range(gram_parts):
         load_gram(k).start()
-    for k in range(hidden - 1):
-        send_part(k).wait_recv()
-
-    for j in range(each):
-        at = pl.ds(j * SEQ, SEQ)
-        left = part[hidden - 1, 0, at, :]
-        right = part[hidden - 1, 1, at, :]
-        for k in range(hidden - 1):
-            left = left + land[k, 0, at, :]
-            right = right + land[k, 1, at, :]
+
+    @pl.when(edge == 0)
+    def _():
+        for j in range(each):
+            part_arrived(relay, j).wait_recv()
+            part[hidden - 2, j] = part[hidden - 2, j] + land[relay, j]
+            part_copy(hidden - 2, j).start()
+
+    def project(j):
+        part_arrived(edge, j).wait_recv()
+        part_arrived(hidden - 1 - edge, j).wait_recv()
+        part[hidden - 1, j] = part[hidden - 1, j] + land[edge, j] + land[hidden - 1 - edge, j]
+
+        @pl.when(edge == 0)
+        def _():
+            part_arrived(hidden - 1 - me, j).wait_recv()
+            part[hidden - 1, j] = part[hidden - 1, j] + land[hidden - 1 - me, j]
+
         proj[j] = lax.dot_general(
-            left,
-            right,
+            part[hidden - 1, j, 0],
+            part[hidden - 1, j, 1],
             (((0,), (0,)), ((), ())),
             precision=lax.Precision.HIGHEST,
             preferred_element_type=jnp.float32,
         )
 
-    mine = (my_col * rep + my_rep) * (hidden * each)
-
-    def send_rows(k):
-        return pltpu.make_async_remote_copy(
-            src_ref=proj.at[:, pl.ds(pl.multiple_of(to(k) * block_p, block_p), block_p), :],
-            dst_ref=allp.at[pl.ds(mine + me * each, each)],
-            send_sem=send2.at[k],
-            recv_sem=recv2.at[k],
+    def place(col, r, z, j):
+        return ((col * rep + r) * hidden + z) * each + j
+
+    def rows_copy(k, j, z):
+        return pltpu.make_async_remote_copy(
+            src_ref=proj.at[j, pl.ds(pl.multiple_of(to(k) * block_p, block_p), block_p), :],
+            dst_ref=allp.at[place(my_col, my_rep, z, j)],
+            send_sem=send2.at[k, j],
+            recv_sem=recv2.at[k, j],
             device_id={"hidden": to(k)},
             device_id_type=MESH,
         )
 
-    def arrived_rows(k):
-        return pltpu.make_async_remote_copy(
-            src_ref=proj.at[:, pl.ds(0, block_p), :],
-            dst_ref=allp.at[pl.ds(mine + source(k) * each, each)],
-            send_sem=send2.at[k],
-            recv_sem=recv2.at[k],
-            device_id={"hidden": to(k)},
-            device_id_type=MESH,
-        )
-
-    for k in range(hidden - 1):
-        send_rows(k).start()
-    for j in range(each):
-        allp[mine + me * each + j] = proj[j, pl.ds(pl.multiple_of(me * block_p, block_p), block_p), :]
-
-    def forward(d, k):
-        c, r = peers[d]
-        block = allp.at[pl.ds(mine + source(k) * each, each)]
+    def col_copy(d, k, j, col):
+        block = allp.at[place(col, my_rep, source(k), j)]
         return pltpu.make_async_remote_copy(
             src_ref=block,
             dst_ref=block,
-            send_sem=send3.at[d, k],
-            recv_sem=recv3.at[d, k],
-            device_id={"cols": lax.rem(my_col + c, cols), "rep": lax.rem(my_rep + r, rep)},
-            device_id_type=MESH,
-        )
-
-    def forwarded(d, k):
-        c, r = peers[d]
-        col = lax.rem(my_col + cols - c, cols)
-        other = (col * rep + lax.rem(my_rep + rep - r, rep)) * (hidden * each)
-        block = allp.at[pl.ds(other + source(k) * each, each)]
+            send_sem=send3.at[d - 1, k, j],
+            recv_sem=recv3.at[d - 1, k, j],
+            device_id={"cols": lax.rem(my_col + d, cols)},
+            device_id_type=MESH,
+        )
+
+    def rep_copy(e, d, k, j, r):
+        block = allp.at[place(lax.rem(my_col + cols - d, cols), r, source(k), j)]
         return pltpu.make_async_remote_copy(
             src_ref=block,
             dst_ref=block,
-            send_sem=send3.at[d, k],
-            recv_sem=recv3.at[d, k],
-            device_id={"cols": col},
-            device_id_type=MESH,
-        )
-
-    for d in range(len(peers)):
-        forward(d, hidden - 1).start()
-    for k in range(hidden - 1):
-        arrived_rows(k).wait_recv()
-        for d in range(len(peers)):
-            forward(d, k).start()
-    for k in range(hidden):
-        for d in range(len(peers)):
-            forwarded(d, k).wait_recv()
+            send_sem=send5.at[e - 1, d, k, j],
+            recv_sem=recv5.at[e - 1, d, k, j],
+            device_id={"rep": lax.rem(my_rep + e, rep)},
+            device_id_type=MESH,
+        )
+
+    def spread(k, j):
+        for d in range(1, cols):
+            col_copy(d, k, j, my_col).start()
+        for e in range(1, rep):
+            rep_copy(e, 0, k, j, my_rep).start()
+
+    def send_rows(j):
+        project(j)
+        for k in range(hidden - 1):
+            rows_copy(k, j, me).start()
+        allp[place(my_col, my_rep, me, j)] = proj[j, pl.ds(pl.multiple_of(me * block_p, block_p), block_p), :]
+        spread(hidden - 1, j)
+
+    def pass_rows(j):
+        for k in range(hidden - 1):
+            rows_copy(k, j, source(k)).wait_recv()
+            spread(k, j)
+
+    def pass_cols(j):
+        for d in range(1, cols):
+            for k in [hidden - 1] + list(range(hidden - 1)):
+                col_copy(d, k, j, lax.rem(my_col + cols - d, cols)).wait_recv()
+                for e in range(1, rep):
+                    rep_copy(e, d, k, j, my_rep).start()
+
+    for j in range(each):
+        send_rows(j)
+        if j > 0:
+            pass_cols(j - 1)
+        pass_rows(j)
+    pass_cols(each - 1)
+    for j in range(each):
+        for k in range(hidden):
+            for d in range(cols):
+                for e in range(1, rep):
+                    rep_copy(e, d, k, j, lax.rem(my_rep + rep - e, rep)).wait_recv()
 
     examples = allp.shape[0]
     for p in range(block_p):
@@ -277,13 +325,18 @@
         total = total + final[k]
     out_ref[...] = total
 
+    for j in range(each):
+        for k in range(hidden - 1):
+            part_copy(k, j).wait_send()
+            rows_copy(k, j, me).wait_send()
+        for k in range(hidden):
+            for d in range(1, cols):
+                col_copy(d, k, j, my_col).wait_send()
+            for d in range(cols):
+                for e in range(1, rep):
+                    rep_copy(e, d, k, j, my_rep).wait_send()
     for k in range(hidden - 1):
-        send_part(k).wait_send()
-        send_rows(k).wait_send()
         send_sum(k).wait_send()
-    for k in range(hidden):
-        for d in range(len(peers)):
-            forward(d, k).wait_send()
 
 
 def fused(dims, inputs, grads, in_signs, out_signs, in_rows, out_rows, inv_gram):
@@ -294,7 +347,6 @@
     block_p = SKETCH // hidden
     examples = count * cols * rep
     share = inv_gram.shape[1] // hidden
-    others = cols * rep - 1
     f32 = jnp.float32
     dma = pltpu.SemaphoreType.DMA
     vmem = pl.BlockSpec(memory_space=pltpu.VMEM)
@@ -311,8 +363,8 @@
             pltpu.VMEM(inv_gram.shape, jnp.bfloat16),
             pltpu.VMEM((inputs.shape[1], SKETCH), jnp.bfloat16),
             pltpu.VMEM((grads.shape[1], SKETCH), jnp.bfloat16),
-            pltpu.VMEM((hidden, 2, tokens, SKETCH), f32),
-            pltpu.VMEM((hidden - 1, 2, tokens, SKETCH), f32),
+            pltpu.VMEM((hidden, each, 2, SEQ, SKETCH), f32),
+            pltpu.VMEM((hidden + 1, each, 2, SEQ, SKETCH), f32),
             pltpu.VMEM((each, SKETCH, SKETCH), f32),
             pltpu.VMEM((examples, block_p, SKETCH), f32),
             pltpu.VMEM((2 * examples, block_p * SKETCH), jnp.bfloat16),
@@ -321,12 +373,14 @@
             dma((hidden,)),
             dma((hidden,)),
             dma((gram_parts,)),
-            dma((hidden - 1,)),
-            dma((hidden - 1,)),
-            dma((hidden - 1,)),
-            dma((hidden - 1,)),
-            dma((others, hidden)),
-            dma((others, hidden)),
+            dma((hidden - 1, each)),
+            dma((hidden + 1, each)),
+            dma((hidden - 1, each)),
+            dma((hidden - 1, each)),
+            dma((max(cols - 1, 1), hidden, each)),
+            dma((max(cols - 1, 1), hidden, each)),
+            dma((max(rep - 1, 1), cols, hidden, each)),
+            dma((max(rep - 1, 1), cols, hidden, each)),
             dma((hidden - 1,)),
             dma((hidden - 1,)),
         ],
@@ -384,7 +438,7 @@
     dims = tuple(mesh.shape[name] for name in ("hidden", "cols", "rep"))
 
     def on_device(inputs, *rest):
-        if inputs.shape[0] % (dims[0] * SEQ) == 0:
+        if dims[0] == 4 and inputs.shape[0] % (dims[0] * SEQ) == 0:
             return fused(dims, inputs, *rest)
         return plain(inputs, *rest)
 

time: 60.4 us -> 56.3 us (0.932)
  Pallas kernels: 57.1 us -> 52.4 us
    pallas_call x1, Pallas kernels: 57.1 us -> 52.4 us  [fused(): pl.pallas_call(functools.partial(fused_kernel, dims), out_shape=jax.Shape...]
where the time goes in v2:
time: 56.3 us; the launch traced here: 55.4 us
  Pallas kernels  52.4 us (93%)
  local copies, waits for them, and re-layouts  3 us (5%)
    pallas_call x1, Pallas kernels, fused(): pl.pallas_call(functools.partial(fused_kernel, dims), out_shape=jax.Shape...  52.4 us
    unnamed x1, local copies, waits for them, and re-layouts  1.57 us
    reshape x1, local copies, waits for them, and re-layouts, fused(): in_signs.reshape(inputs.shape[1] // (IN_W // HAD), IN_W // HAD)  1.44 us

profile of v2, /device:TPU:0, one launch (start us, length us, event | category | flops | bytes accessed | tf_op | source)
XLA Modules:
  0.0 55.4 jit_solution(12634580226845325354)
XLA Ops:
  0.0 1.4 %reshape.12.in_sign_ref = s32[16,448]{1,0:T(8,128)} reshape(s32[7168]{0:T(1024)} %param.9) | data formatting | bytes 57344 | tf_op jit(solution)/shard_map/reshape | solution.py:393
  1.4 52.4 %shard_map.73 = f32[32,1024]{1,0:T(8,128)} custom-call(bf16[1024,7168]{1,0:T(8,128)(2,1)} %x_ref.1, bf16[1024,2048]{1,0:T(8,128)(2,1)} %g_ref.1, s32[16,448]{1,0:T(8,128)} %reshape.12.in_sign_ref, s32[16,128]{1,0:T(8,128)} %bitcast.3, s32[1,128]{1,0:T(1,128)} %bitcast.4, s32[1,128]{1,0:T(1,128)} %bitcast.5, bf16[4096,4096]{1,0:T(8,128)(2,1)} %gram_ref.1), custom_call_target="tpu_custom_call" | custom-call | tf_op jit(solution)/shard_map/pallas_call | solution.py:355
  53.8 1.6 %copy.9 = f32[32,1024]{1,0:T(8,128)} copy(f32[32,1024]{1,0:T(8,128)} %shard_map.73) | data formatting | bytes 262144

commit v3 on v2

--- a/solution.py
+++ b/solution.py
@@ -13,6 +13,7 @@
 HAD = 64
 SKETCH = 128
 SEQ = 128
+LANES = 128
 MESH = pl.DeviceIdType.MESH
 
 
@@ -30,20 +31,25 @@
 
 def build_matrix(rows_ref, sign_ref, out_ref, shard, width):
     inner = width // HAD
-    local_high = sign_ref.shape[0]
+    local_high = out_ref.shape[0] // inner
     high, low = split_rows(rows_ref[...], inner)
     hit = lax.broadcasted_iota(jnp.int32, (inner, SKETCH), 0) == low
     onehot = jnp.where(hit, 1.0, 0.0)
-    picked = jnp.dot(
-        sign_ref[...].astype(jnp.bfloat16),
-        onehot.astype(jnp.bfloat16),
-        preferred_element_type=jnp.float32,
-    )
-    sources = shard * local_high + lax.broadcasted_iota(jnp.int32, (local_high, SKETCH), 0)
-    parity = had_parity(jnp.broadcast_to(high, (local_high, SKETCH)), sources)
-    coef = picked * (1 - 2 * parity).astype(jnp.float32) * (1.0 / math.sqrt(HAD))
+    sign = sign_ref[...].astype(jnp.float32).astype(jnp.bfloat16)
+    line = lax.broadcasted_iota(jnp.int32, (sign.shape[0], SKETCH), 0)
+    lane = lax.broadcasted_iota(jnp.int32, (LANES, SKETCH), 0)
+    picked = {}
     for h in range(local_high):
-        out_ref[h * inner : (h + 1) * inner, :] = (onehot * coef[h : h + 1, :]).astype(jnp.bfloat16)
+        first, offset = divmod(h * inner, LANES)
+        at = offset + low
+        if offset not in picked:
+            pick = jnp.where(lane == jnp.bitwise_and(at, LANES - 1), 1.0, 0.0).astype(jnp.bfloat16)
+            picked[offset] = jnp.dot(sign, pick, preferred_element_type=jnp.float32)
+        own = line == first + jnp.right_shift(at, LANES.bit_length() - 1)
+        coef = jnp.sum(jnp.where(own, picked[offset], 0.0), axis=0, keepdims=True)
+        parity = had_parity(high, shard * local_high + h)
+        coef = coef * (1 - 2 * parity).astype(jnp.float32) * (1.0 / math.sqrt(HAD))
+        out_ref[h * inner : (h + 1) * inner, :] = (onehot * coef).astype(jnp.bfloat16)
 
 
 def fused_kernel(
@@ -291,39 +297,60 @@
     for k in range(gram_parts):
         load_gram(k).wait()
 
-    share = psum.shape[2]
-    step = 256
-    per = share // step
-
-    def send_sum(k):
-        return pltpu.make_async_remote_copy(
-            src_ref=psum.at[k],
-            dst_ref=final.at[k],
-            send_sem=send4.at[k],
-            recv_sem=recv4.at[k],
-            device_id={"hidden": to(k)},
+    per, step = psum.shape[1], psum.shape[3]
+
+    def sum_copy(s, c):
+        passed = edge * (1 - (s + hidden - 1) // hidden)
+        slot = me + passed * (relay - me)
+        dest = target(s)
+        return pltpu.make_async_remote_copy(
+            src_ref=psum.at[s, c],
+            dst_ref=final.at[slot, c],
+            send_sem=send4.at[s, c],
+            recv_sem=recv4.at[slot, c],
+            device_id={"hidden": dest + passed * (1 + half - dest)},
+            device_id_type=MESH,
+        )
+
+    def sum_arrived(slot, c):
+        return pltpu.make_async_remote_copy(
+            src_ref=psum.at[0, c],
+            dst_ref=final.at[slot, c],
+            send_sem=send4.at[0, c],
+            recv_sem=recv4.at[slot, c],
+            device_id={"hidden": to(0)},
             device_id_type=MESH,
         )
 
     def gram_step(n, carry):
-        k = n // per
-        at = pl.multiple_of(lax.rem(n, per) * step, step)
-        column = pl.multiple_of(to(k) * share + at, step)
+        s = n // per
+        c = lax.rem(n, per)
+        column = pl.multiple_of((target(s) * per + c) * step, step)
         both = jnp.dot(wide[...], gram_buf[:, pl.ds(column, step)], preferred_element_type=jnp.float32)
-        psum[k, :, pl.ds(at, step)] = both[:examples] + both[examples:]
-
-        @pl.when(jnp.logical_and(lax.rem(n, per) == per - 1, k < hidden - 1))
+        psum[s, c] = both[:examples] + both[examples:]
+
+        @pl.when(s < hidden - 2 + edge)
         def _():
-            send_sum(k).start()
+            sum_copy(s, c).start()
 
         return carry
 
     lax.fori_loop(0, hidden * per, gram_step, 0)
-    total = psum[hidden - 1]
-    for k in range(hidden - 1):
-        send_sum(k).wait_recv()
-        total = total + final[k]
-    out_ref[...] = total
+
+    @pl.when(edge == 0)
+    def _():
+        for c in range(per):
+            sum_arrived(relay, c).wait_recv()
+            psum[hidden - 2, c] = psum[hidden - 2, c] + final[relay, c]
+            sum_copy(hidden - 2, c).start()
+        for c in range(per):
+            sum_arrived(hidden - 1 - me, c).wait_recv()
+            psum[hidden - 1, c] = psum[hidden - 1, c] + final[hidden - 1 - me, c]
+
+    for c in range(per):
+        sum_arrived(edge, c).wait_recv()
+        sum_arrived(hidden - 1 - edge, c).wait_recv()
+        out_ref[:, c * step : (c + 1) * step] = psum[hidden - 1, c] + final[edge, c] + final[hidden - 1 - edge, c]
 
     for j in range(each):
         for k in range(hidden - 1):
@@ -336,7 +363,8 @@
                 for e in range(1, rep):
                     rep_copy(e, d, k, j, my_rep).wait_send()
     for k in range(hidden - 1):
-        send_sum(k).wait_send()
+        for c in range(per):
+            sum_copy(k, c).wait_send()
 
 
 def fused(dims, inputs, grads, in_signs, out_signs, in_rows, out_rows, inv_gram):
@@ -347,6 +375,7 @@
     block_p = SKETCH // hidden
     examples = count * cols * rep
     share = inv_gram.shape[1] // hidden
+    per = share // 256
     f32 = jnp.float32
     dma = pltpu.SemaphoreType.DMA
     vmem = pl.BlockSpec(memory_space=pltpu.VMEM)
@@ -368,8 +397,8 @@
             pltpu.VMEM((each, SKETCH, SKETCH), f32),
             pltpu.VMEM((examples, block_p, SKETCH), f32),
             pltpu.VMEM((2 * examples, block_p * SKETCH), jnp.bfloat16),
-            pltpu.VMEM((hidden, examples, share), f32),
-            pltpu.VMEM((hidden - 1, examples, share), f32),
+            pltpu.VMEM((hidden, per, examples, share // per), f32),
+            pltpu.VMEM((hidden + 1, per, examples, share // per), f32),
             dma((hidden,)),
             dma((hidden,)),
             dma((gram_parts,)),
@@ -381,8 +410,8 @@
             dma((max(cols - 1, 1), hidden, each)),
             dma((max(rep - 1, 1), cols, hidden, each)),
             dma((max(rep - 1, 1), cols, hidden, each)),
-            dma((hidden - 1,)),
-            dma((hidden - 1,)),
+            dma((hidden - 1, per)),
+            dma((hidden + 1, per)),
         ],
         compiler_params=pltpu.CompilerParams(
             collective_id=0, has_side_effects=True, vmem_limit_bytes=63 << 20
@@ -390,8 +419,8 @@
     )(
         inputs,
         grads,
-        in_signs.reshape(inputs.shape[1] // (IN_W // HAD), IN_W // HAD),
-        out_signs.reshape(grads.shape[1] // (OUT_W // HAD), OUT_W // HAD),
+        in_signs.reshape(inputs.shape[1] // LANES, LANES),
+        out_signs.reshape(grads.shape[1] // LANES, LANES),
         in_rows.reshape(1, SKETCH),
         out_rows.reshape(1, SKETCH),
         inv_gram,

time: 56.3 us -> 53.9 us (0.957); the launches traced: 55.4 us -> 53.7 us
  local copies, waits for them, and re-layouts: 3 us -> 1.57 us
    reshape x1 -> x0, local copies, waits for them, and re-layouts: 1.44 us -> none  [fused(): in_signs.reshape(inputs.shape[1] // (IN_W // HAD), IN_W // HAD)]
where the time goes in v3:
time: 53.9 us; the launch traced here: 53.7 us
  Pallas kernels  52.2 us (97%)
  local copies, waits for them, and re-layouts  1.57 us (3%)
    pallas_call x1, Pallas kernels, fused(): pl.pallas_call(functools.partial(fused_kernel, dims), out_shape=jax.Shape...  52.2 us
    unnamed x1, local copies, waits for them, and re-layouts  1.57 us

profile of v3, /device:TPU:0, one launch (start us, length us, event | category | flops | bytes accessed | tf_op | source)
XLA Modules:
  0.0 53.7 jit_solution(1526554337671840152)
XLA Ops:
  0.0 52.2 %shard_map.73 = f32[32,1024]{1,0:T(8,128)} custom-call(bf16[1024,7168]{1,0:T(8,128)(2,1)} %x_ref.1, bf16[1024,2048]{1,0:T(8,128)(2,1)} %g_ref.1, s32[56,128]{1,0:T(8,128)} %bitcast.4, s32[16,128]{1,0:T(8,128)} %bitcast.5, s32[1,128]{1,0:T(1,128)} %bitcast.6, s32[1,128]{1,0:T(1,128)} %bitcast.7, bf16[4096,4096]{1,0:T(8,128)(2,1)} %gram_ref.1), custom_call_target="tpu_custom_call" | custom-call | tf_op jit(solution)/shard_map/pallas_call | solution.py:384
  52.2 1.6 %copy.9 = f32[32,1024]{1,0:T(8,128)} copy(f32[32,1024]{1,0:T(8,128)} %shard_map.73) | data formatting | bytes 262144

commit v4 on v3

--- a/solution.py
+++ b/solution.py
@@ -350,7 +350,9 @@
     for c in range(per):
         sum_arrived(edge, c).wait_recv()
         sum_arrived(hidden - 1 - edge, c).wait_recv()
-        out_ref[:, c * step : (c + 1) * step] = psum[hidden - 1, c] + final[edge, c] + final[hidden - 1 - edge, c]
+        at = pl.ds(c * step, step)
+        out_ref[0, :, at] = psum[hidden - 1, c] + final[edge, c]
+        out_ref[1, :, at] = final[hidden - 1 - edge, c]
 
     for j in range(each):
         for k in range(hidden - 1):
@@ -381,9 +383,9 @@
     vmem = pl.BlockSpec(memory_space=pltpu.VMEM)
     hbm = pl.BlockSpec(memory_space=pl.ANY)
     gram_parts = 4
-    return pl.pallas_call(
+    terms = pl.pallas_call(
         functools.partial(fused_kernel, dims),
-        out_shape=jax.ShapeDtypeStruct((examples, share), f32),
+        out_shape=jax.ShapeDtypeStruct((2, examples, share), f32),
         in_specs=[hbm, hbm, vmem, vmem, vmem, vmem, hbm],
         out_specs=vmem,
         scratch_shapes=[
@@ -425,6 +427,7 @@
         out_rows.reshape(1, SKETCH),
         inv_gram,
     )
+    return terms[0] + terms[1]
 
 
 def plain_sketch(values, signs, rows, width, shard):

time: 53.9 us -> 54.1 us (level)
  other arithmetic: 0 us -> 1.64 us
  local copies, waits for them, and re-layouts: 1.57 us -> 0 us
    add x0 -> x1, other arithmetic: none -> 1.64 us  [fused(): return terms[0] + terms[1]]
    unnamed x1 -> x0, local copies, waits for them, and re-layouts: 1.57 us -> none
where the time goes in v4:
time: 54.1 us; the launch traced here: 53.9 us
  Pallas kernels  52.2 us (96%)
  other arithmetic  1.64 us (3%)
    pallas_call x1, Pallas kernels, fused(): pl.pallas_call(functools.partial(fused_kernel, dims), out_shape=jax.Shape...  52.2 us
    add x1, other arithmetic, fused(): return terms[0] + terms[1]  1.64 us

profile of v4, /device:TPU:0, one launch (start us, length us, event | category | flops | bytes accessed | tf_op | source)
XLA Modules:
  0.0 53.9 jit_solution(1530546493015381925)
XLA Ops:
  0.0 52.2 %shard_map.73 = f32[2,32,1024]{2,1,0:T(8,128)} custom-call(bf16[1024,7168]{1,0:T(8,128)(2,1)} %x_ref.1, bf16[1024,2048]{1,0:T(8,128)(2,1)} %g_ref.1, s32[56,128]{1,0:T(8,128)} %bitcast.6, s32[16,128]{1,0:T(8,128)} %bitcast.7, s32[1,128]{1,0:T(1,128)} %bitcast.8, s32[1,128]{1,0:T(1,128)} %bitcast.9, bf16[4096,4096]{1,0:T(8,128)(2,1)} %gram_ref.1), custom_call_target="tpu_custom_call" | custom-call | tf_op jit(solution)/shard_map/pallas_call | solution.py:386
  52.2 1.6 %add_bitcast_fusion = f32[32,1024]{1,0:T(8,128)} fusion(f32[2,32,1024]{2,1,0:T(8,128)} %shard_map.73), kind=kLoop, calls=%fused_computation | loop fusion | flops 32768 | bytes 393216 | tf_op jit(solution)/shard_map/add | solution.py:430
